TPU v7x, 32 devices: a whole 2x2x4 slice. The times are simulated.
32 devices in a mesh: outer: 4 (over z), inner: 2 (over y), head: 4 (over x, core).
Axes of the slice: x: 2, y: 2, z: 4, core: 2. Of those that a mesh axis runs over, the one named last changes fastest.
Arguments:
- values: bfloat16 [8192, 4096], P(('outer', 'inner'), 'head'), may hold values from -40 to 40
- input_state: bfloat16 [8192, 128], P(('outer', 'inner')), may hold values from -0.5 to 0.5
- output_state: bfloat16 [8192, 128], P(('outer', 'inner')), may hold values from -6 to 6
- step_log_decay: float32 [64, 8192], P('head', ('outer', 'inner')), may hold values from -0.6 to 0
- level_gates: float32 [4, 64, 8192], P(None, 'head', ('outer', 'inner')), may hold values from 0.1 to 1
- norm_gain: float32 [4096], P('head'), may hold values from 0.25 to 1.75
Outputs:
- mixed: bfloat16 [8192, 4096], P(('outer', 'inner'), 'head')
All inputs are finite; a program needn't handle non-finite values.
Results may differ from a plain program's by a relative error of at most 0.0051.
Values sent between devices are 32-bit elements; how exact they have to be, the bound alone decides.
A program may use at most 64 MiB of HBM per device.

v0:
```python
import jax
import jax.numpy as jnp
from jax import lax
from jax.sharding import PartitionSpec as P

P_SIZE = 64
N = 128
SPAN = 256


def partner_2(array, axis, bit):
    return lax.ppermute(array, axis, [(i, i ^ 1 << bit) for i in range(lax.axis_size(axis))])


def piece_scan(values, in_rows, out_rows, log_decay):
    tokens = values.shape[0]
    width_all = values.shape[1]
    head_count = log_decay.shape[0]
    piece_count = tokens // SPAN
    causal = jnp.arange(SPAN)[:, None] >= jnp.arange(SPAN)[None, :]
    block_state = jnp.zeros((head_count, P_SIZE, N), jnp.float32)
    offset = jnp.zeros((head_count,), jnp.float32)
    zero_parts = []
    cum_parts = []
    for piece in range(piece_count):
        first = piece * SPAN
        val_piece = values[first : first + SPAN].reshape(SPAN, head_count, P_SIZE)
        in_piece = in_rows[first : first + SPAN]
        out_piece = out_rows[first : first + SPAN]
        running = jnp.cumsum(log_decay[:, first : first + SPAN], axis=1)
        piece_total = running[:, -1]
        weighted = (in_piece[None] * jnp.exp(piece_total[:, None] - running)[:, :, None]).astype(
            jnp.bfloat16
        )
        fresh_state = jnp.einsum(
            "shp,hsn->hpn", val_piece, weighted, preferred_element_type=jnp.float32
        )
        scores = jnp.dot(out_piece, in_piece.T, preferred_element_type=jnp.float32)
        spread = running[:, :, None] - running[:, None, :]
        fading = jnp.exp(jnp.where(causal[None], spread, -jnp.inf))
        mixing = (scores[None] * fading).astype(jnp.bfloat16)
        within = jnp.einsum(
            "hts,shp->thp", mixing, val_piece, preferred_element_type=jnp.float32
        ).reshape(SPAN, width_all)
        earlier = jnp.einsum(
            "tn,hpn->thp",
            out_piece,
            block_state.astype(jnp.bfloat16),
            preferred_element_type=jnp.float32,
        ).reshape(SPAN, width_all)
        zero_parts.append(within + earlier * jnp.repeat(jnp.exp(running).T, P_SIZE, axis=1))
        cum_parts.append(running + offset[:, None])
        block_state = jnp.exp(piece_total)[:, None, None] * block_state + fresh_state
        offset = offset + piece_total
    return (
        block_state,
        offset,
        jnp.concatenate(zero_parts, axis=0),
        jnp.concatenate(cum_parts, axis=1),
    )


def merge_pair(lower_side, upper_side):
    return (
        jnp.exp(upper_side[1])[:, None, None] * lower_side[0] + upper_side[0],
        lower_side[1] + upper_side[1],
    )


def swap_levels(aggregate, position, level_count, running_gap, partner):
    buckets = []
    gap_list = []
    upper_flags = []
    for step_bit in range(level_count):
        partner_agg = lax.optimization_barrier(partner(aggregate, step_bit))
        upper_flag = jnp.bitwise_and(jnp.right_shift(position, step_bit), 1).astype(jnp.float32)
        buckets.append(partner_agg[0])
        gap_list.append(running_gap)
        upper_flags.append(upper_flag)
        running_gap = running_gap + upper_flag * partner_agg[1]
        is_upper = upper_flag > 0
        lower_side = (
            jnp.where(is_upper, partner_agg[0], aggregate[0]),
            jnp.where(is_upper, partner_agg[1], aggregate[1]),
        )
        upper_side = (
            jnp.where(is_upper, aggregate[0], partner_agg[0]),
            jnp.where(is_upper, aggregate[1], partner_agg[1]),
        )
        aggregate = merge_pair(lower_side, upper_side)
    return (buckets, gap_list, upper_flags, running_gap, aggregate)


def far_terms(out_rows, buckets, gap_list, upper_flags, upper_gates, cum):
    stacked = jnp.stack(buckets)
    level_count, head_count, head_width, state_size = stacked.shape
    products = jnp.einsum(
        "tn,lkn->ltk",
        out_rows.astype(jnp.float32),
        stacked.reshape(level_count, head_count * head_width, state_size),
        precision=lax.Precision.HIGHEST,
        preferred_element_type=jnp.float32,
    )
    weights = (
        upper_gates
        * jnp.stack(upper_flags)[:, None, None]
        * jnp.exp(cum[None] + jnp.stack(gap_list)[:, :, None])
    )
    wide_weights = jnp.repeat(jnp.transpose(weights, (0, 2, 1)), head_width, axis=2)
    return jnp.sum(products * wide_weights, axis=0)


def per_device(values, input_state, output_state, step_log_decay, level_gates, norm_gain):
    tokens = values.shape[0]
    width_all = values.shape[1]
    head_count = step_log_decay.shape[0]
    block_state, block_log, level_zero, cum = piece_scan(
        values, input_state, output_state, step_log_decay
    )
    zero_gap = jnp.zeros((head_count,), jnp.float32)
    swap_result = swap_levels(
        (block_state, block_log),
        lax.axis_index(("outer", "inner")),
        lax.axis_size(("outer", "inner")).bit_length() - 1,
        zero_gap,
        lambda pieces, step_bit: partner_2(pieces, ("outer", "inner"), step_bit),
    )
    buckets, gap_list, upper_flags = (swap_result[0], swap_result[1], swap_result[2])
    gate_wide = jnp.repeat(level_gates[0].T, P_SIZE, axis=1)
    combined = gate_wide * level_zero + far_terms(
        output_state, buckets, gap_list, upper_flags, level_gates[1:], cum
    )
    mean_square = jnp.mean((combined * combined).reshape(tokens, head_count, P_SIZE), axis=2)
    scale_wide = jnp.repeat(lax.rsqrt(mean_square + 1e-05), P_SIZE, axis=1)
    return (combined * scale_wide * norm_gain[None, :]).astype(jnp.bfloat16)


def solution(mesh):
    placed = (
        P(("outer", "inner"), "head"),
        P(("outer", "inner"), None),
        P(("outer", "inner"), None),
        P("head", ("outer", "inner")),
        P(None, "head", ("outer", "inner")),
        P("head"),
    )
    return jax.shard_map(
        per_device,
        mesh=mesh,
        in_specs=placed,
        out_specs=P(("outer", "inner"), "head"),
        check_vma=False,
    )
```

profile of v0, /device:TPU:0, one launch (start us, length us, event | category | flops | bytes accessed | tf_op | source)
XLA Modules:
  0.0 94.3 jit_solution(9569759580483232599)
XLA Ops:
  0.0 0.8 slice_bitcast_fusion.2
  0.8 0.6 reduce-window.36
  1.6 0.6 reduce-window.34
  2.7 0.4 copy-done.19
  3.1 0.6 reduce-window.30
  3.9 0.6 reduce-window.26
  4.8 0.3 fusion.86
  5.1 0.6 add_add_fusion
  5.7 3.0 %collective-permute-start.1 = (f32[16]{0:T(128)}, f32[16]{0:T(128)}, u32[]{:S(2)}, u32[]{:S(2)}) collective-permute-start(f32[16]{0:T(128)} %get-tuple-element.46), channel_id=1, source_target_pairs={{0,4},{4,0},{8,12},{12,8},{16,20},{20,16},{24,28},{28,24},{1,5},{5... | collective-permute-start | bytes 200 | tf_op jit(solution)/shard_map/ppermute | solution.py:12
  8.6 0.7 exponential_bitcast_fusion.3
  9.3 0.7 exponential_bitcast_fusion.2
  10.0 0.7 exponential_bitcast_fusion.1
  10.7 0.7 exponential_bitcast_fusion
  11.4 1.7 %slice_convert_fusion.3 = (f32[256,128]{1,0:T(8,128)}, f32[256,128]{1,0:T(8,128)}, f32[256,128]{1,0:T(8,128)S(1)}, f32[256,128]{1,0:T(8,128)S(1)}) fusion(bf16[1024,128]{1,0:T(8,128)(2,1)} %param.7), kind=kLoop, calls=%fused_computation.111 | loop fusion | flops 131072 | bytes 786432 | tf_op jit(solution)/shard_map/convert_element_type | solution.py:32
  13.1 1.7 %fusion.96 = (bf16[256,1024]{1,0:T(8,128)(2,1)S(1)}, bf16[256,1024]{1,0:T(8,128)(2,1)S(1)}, bf16[256,1024]{1,0:T(8,128)(2,1)S(1)}, bf16[256,1024]{1,0:T(8,128)(2,1)S(1)}) fusion(bf16[1024,1024]{1,0:T(8,128)(2,1)} %param.6), kind=kLoop, calls=%fused_computation.172 | loop fusion | bytes 4194304 | tf_op jit(solution)/shard_map/slice | solution.py:27
  14.8 0.2 copy.53
  15.7 1.7 %convolution_add_fusion.3 = f32[16,128,64]{1,2,0:T(8,128)S(1)} fusion(bf16[256,16,64]{0,2,1:T(8,128)(2,1)S(1)} %bitcast.184, f32[16,256]{1,0:T(8,128)} %get-tuple-element.31, f32[256,128]{1,0:T(8,128)} %get-tuple-element.22, f32[16]{0:T(128)} %get-tuple-element.48), kind=kOutput, calls=%fused_computation.68 | convolution fusion | flops 68288512 | bytes 1196096 | tf_op jit(solution)/shard_map/shp,hsn->hpn/dot_general | solution.py:35
  17.4 1.7 %convolution_add_fusion.2 = f32[16,128,64]{1,2,0:T(8,128)S(1)} fusion(bf16[256,16,64]{0,2,1:T(8,128)(2,1)S(1)} %bitcast.179, f32[16,256]{1,0:T(8,128)} %get-tuple-element.34, f32[256,128]{1,0:T(8,128)} %get-tuple-element.23, f32[16,128,64]{1,2,0:T(8,128)S(1)} %convolution_add_fusion.3, f32[16]{0:T(128)} %get-tuple-element.47), kind=kOutput, calls=%fused_computation.67 | convolution fusion | flops 68419584 | bytes 1720384 | tf_op jit(solution)/shard_map/shp,hsn->hpn/dot_general | solution.py:35
  19.1 1.6 %convolution_add_fusion.1 = f32[16,128,64]{1,2,0:T(8,128)S(1)} fusion(bf16[256,16,64]{0,2,1:T(8,128)(2,1)S(1)} %bitcast.181, f32[16,256]{1,0:T(8,128)} %get-tuple-element.37, f32[256,128]{1,0:T(8,128)S(1)} %get-tuple-element.24, f32[16,128,64]{1,2,0:T(8,128)S(1)} %convolution_add_fusion.2, f32[16]{0:T(128)} %get-tuple-element.49), kind=kOutput, calls=%fused_computation.66 | convolution fusion | flops 68419584 | bytes 1720384 | tf_op jit(solution)/shard_map/shp,hsn->hpn/dot_general | solution.py:35
  20.7 0.8 copy-done
  21.5 2.4 %fusion.49 = f32[16,64,128]{2,1,0:T(8,128)} fusion(bf16[256,16,64]{0,2,1:T(8,128)(2,1)S(1)} %bitcast.177, f32[16,256]{1,0:T(8,128)} %get-tuple-element.40, f32[256,128]{1,0:T(8,128)S(1)} %get-tuple-element.25, f32[16,128,64]{1,2,0:T(8,128)S(1)} %convolution_add_fusion.1, f32[16]{0:T(128)} %get-tuple-element.50), kind=kOutput, calls=%fused_computation.65 | convolution fusion | flops 68419584 | bytes 1720384 | tf_op jit(solution)/shard_map/shp,hsn->hpn/dot_general | solution.py:35
  23.9 0.9 fusion.78
  24.8 0.9 fusion.82
  25.7 0.9 fusion.74
  26.6 2.1 %fusion.40 = f32[256,16,64]{0,2,1:T(8,128)S(1)} fusion(bf16[256,16,64]{0,2,1:T(8,128)(2,1)S(1)} %bitcast.185, f32[16,256]{1,0:T(8,128)S(1)} %copy_bitcast_fusion.3, f32[256,256]{1,0:T(8,128)} %fusion.82, pred[256,256]{1,0:T(8,128)(4,1)S(1)} %iota_compare_fusion), kind=kOutput, calls=%fused_computation.51 | convolution fusion | flops 138412032 | bytes 1916928 | tf_op jit(solution)/shard_map/hts,shp->thp/dot_general | solution.py:42
  28.7 1.1 %fusion.39 = f32[256,16,64]{0,2,1:T(8,128)S(1)} fusion(bf16[256,16,64]{0,2,1:T(8,128)(2,1)S(1)} %bitcast.180, f32[16,256]{1,0:T(8,128)S(1)} %copy-done.24, f32[256,256]{1,0:T(8,128)S(1)} %copy-done.9, pred[256,256]{1,0:T(8,128)(4,1)S(1)} %iota_compare_fusion), kind=kOutput, calls=%fused_computation.50 | convolution fusion | flops 138412032 | bytes 1916928 | tf_op jit(solution)/shard_map/hts,shp->thp/dot_general | solution.py:42
  29.9 1.1 %fusion.38 = f32[256,16,64]{0,2,1:T(8,128)S(1)} fusion(bf16[256,16,64]{0,2,1:T(8,128)(2,1)S(1)} %bitcast.182, f32[16,256]{1,0:T(8,128)S(1)} %copy-done.22, f32[256,256]{1,0:T(8,128)S(1)} %copy-done.8, pred[256,256]{1,0:T(8,128)(4,1)S(1)} %iota_compare_fusion), kind=kOutput, calls=%fused_computation.49 | convolution fusion | flops 138412032 | bytes 1916928 | tf_op jit(solution)/shard_map/hts,shp->thp/dot_general | solution.py:42
  31.0 0.3 fusion.42
  31.3 0.3 fusion.44
  31.6 0.3 fusion.46
  31.9 1.0 %fusion.70 = f32[256,256]{1,0:T(8,128)S(1)} fusion(bf16[1024,128]{1,0:T(8,128)(2,1)} %param.7, bf16[1024,128]{1,0:T(8,128)(2,1)S(1)} %copy-done.3), kind=kOutput, calls=%fused_computation.97 | convolution fusion | flops 16777216 | bytes 393216 | tf_op jit(solution)/shard_map/dot_general | solution.py:38
  33.0 2.2 %fusion.37 = f32[256,16,64]{0,2,1:T(8,128)} fusion(bf16[256,16,64]{0,2,1:T(8,128)(2,1)S(1)} %bitcast.178, f32[16,256]{1,0:T(8,128)S(1)} %copy-done.20, f32[256,256]{1,0:T(8,128)S(1)} %fusion.70, pred[256,256]{1,0:T(8,128)(4,1)S(1)} %copy-done.15), kind=kOutput, calls=%fused_computation.48 | convolution fusion | flops 138412032 | bytes 1916928 | tf_op jit(solution)/shard_map/hts,shp->thp/dot_general | solution.py:42
  35.2 2.3 %collective-permute-done = f32[16,64,128]{2,1,0:T(8,128)} collective-permute-done((f32[16,64,128]{2,1,0:T(8,128)}, f32[16,64,128]{2,1,0:T(8,128)}, u32[]{:S(2)}, u32[]{:S(2)}) %collective-permute-start) | collective-permute-done | bytes 524320 | tf_op jit(solution)/shard_map/ppermute | solution.py:12
  37.5 1.2 %fusion.87 = (f32[16]{0:T(128)}, f32[16]{0:T(128)S(1)}) fusion(f32[16]{0:T(128)} %collective-permute-done.1, f32[16]{0:T(128)} %get-tuple-element.46, pred[]{:T(512)S(6)} %gt.6), kind=kLoop, calls=%fused_computation.158 | loop fusion | flops 48 | bytes 257 | tf_op jit(solution)/shard_map/add | solution.py:66
  38.7 2.1 %select_add_fusion.1 = f32[16,64,128]{2,1,0:T(8,128)} fusion(f32[16,64,128]{2,1,0:T(8,128)} %fusion.49, f32[16,64,128]{2,1,0:T(8,128)} %collective-permute-done, f32[16]{0:T(128)S(1)} %get-tuple-element.42, pred[]{:T(512)S(6)} %gt.6), kind=kLoop, calls=%fused_computation.78 | loop fusion | flops 524288 | bytes 1572929 | tf_op jit(solution)/shard_map/add | solution.py:65
  40.9 1.6 %collective-permute-start.2 = (f32[16,64,128]{2,1,0:T(8,128)}, f32[16,64,128]{2,1,0:T(8,128)}, u32[]{:S(2)}, u32[]{:S(2)}) collective-permute-start(f32[16,64,128]{2,1,0:T(8,128)} %select_add_fusion.1), channel_id=1, source_target_pairs={{0,8},{4,12},{8,0},{12,4},{16,24},{20,28},{24,16},{28,20},{1,9},{5... | collective-permute-start | bytes 1572872 | tf_op jit(solution)/shard_map/ppermute | solution.py:12
  42.5 0.9 slice_bitcast_fusion
  43.4 1.7 %fusion.48 = f32[256,16,64]{0,2,1:T(8,128)S(1)} fusion(f32[256,16,64]{0,2,1:T(8,128)} %fusion.37, f32[256,16]{0,1:T(8,128)S(1)} %copy-done.11, f32[16,128,64]{1,2,0:T(8,128)} %copy-done, bf16[1024,128]{1,0:T(8,128)(2,1)S(1)} %copy-done.3), kind=kOutput, calls=%fused_computation.63 | convolution fusion | flops 67764224 | bytes 2703360 | tf_op jit(solution)/shard_map/tn,hpn->thp/dot_general | solution.py:45
  45.1 0.5 collective-permute-start.3
  45.6 8.1 %collective-permute-done.3 = f32[16]{0:T(128)S(1)} collective-permute-done((f32[16]{0:T(128)}, f32[16]{0:T(128)S(1)}, u32[]{:S(2)}, u32[]{:S(2)}) %collective-permute-start.3) | collective-permute-done | bytes 96 | tf_op jit(solution)/shard_map/ppermute | solution.py:12
  53.7 0.7 fusion.88
  54.3 1.3 %select_add_fusion = f32[16,64,128]{2,1,0:T(8,128)S(1)} fusion(f32[16,64,128]{2,1,0:T(8,128)} %select_add_fusion.1, f32[16,64,128]{2,1,0:T(8,128)} %collective-permute-done.2, f32[16]{0:T(128)S(1)} %get-tuple-element.43, pred[]{:T(512)S(6)} %gt.7), kind=kLoop, calls=%fused_computation.77 | loop fusion | flops 524288 | bytes 1572929 | tf_op jit(solution)/shard_map/add | solution.py:65
  55.7 2.7 %collective-permute-start.4 = (f32[16,64,128]{2,1,0:T(8,128)S(1)}, f32[16,64,128]{2,1,0:T(8,128)S(1)}, u32[]{:S(2)}, u32[]{:S(2)}) collective-permute-start(f32[16,64,128]{2,1,0:T(8,128)S(1)} %select_add_fusion), channel_id=1, source_target_pairs={{0,16},{4,20},{8,24},{12,28},{16,0},{20,4},{24,8},{28,12},{1,17},{... | collective-permute-start | bytes 1572872 | tf_op jit(solution)/shard_map/ppermute | solution.py:12
  58.6 20.8 %collective-permute-done.4 = f32[16,64,128]{2,1,0:T(8,128)S(1)} collective-permute-done((f32[16,64,128]{2,1,0:T(8,128)S(1)}, f32[16,64,128]{2,1,0:T(8,128)S(1)}, u32[]{:S(2)}, u32[]{:S(2)}) %collective-permute-start.4) | collective-permute-done | bytes 524320 | tf_op jit(solution)/shard_map/ppermute | solution.py:12
  79.4 7.7 %fusion = f32[1024,1024]{0,1:T(8,128)S(1)} fusion(f32[3,1024,16]{1,2,0:T(8,128)S(1)} %multiply_bitcast_fusion, f32[1,1024,128]{2,1,0:T(8,128)S(1)} %bitcast.183, f32[1,1024,128]{2,1,0:T(8,128)} %bitcast.32, f32[1,1024,128]{2,1,0:T(8,128)} %bitcast.31, bf16[1024,128]{1,0:T(8,128)(2,1)S(1)} %copy-done.3), kind=kOutput, calls=%fused_computation.1 | convolution fusion | flops 4837867520 | bytes 6225920 | tf_op jit(solution)/shard_map/tn,lkn->ltk/dot_general | solution.py:97
  87.1 1.0 %fusion.7 = f32[1024,16]{0,1:T(8,128)S(1)} fusion(f32[256,16,64]{0,2,1:T(8,128)S(1)} %fusion.48, f32[256,16,64]{0,2,1:T(8,128)S(1)} %fusion.46, f32[256,16,64]{0,2,1:T(8,128)S(1)} %fusion.44, f32[256,16,64]{0,2,1:T(8,128)S(1)} %fusion.42, f32[1024,16]{0,1:T(8,128)S(1)} %slice_bitcast_fusion, f32[1024,1024]{0,1:T(8,128)S(1)} %fusion), kind=kLoop, calls=%fused_computation.10 | loop fusion | flops 7323648 | bytes 8519680 | tf_op jit(solution)/shard_map/reduce_sum | solution.py:133
  88.2 2.2 %fusion.4 = bf16[1024,1024]{0,1:T(8,128)(2,1)} fusion(f32[1024,1024]{0,1:T(8,128)S(1)} %fusion, f32[256,1024]{0,1:T(8,128)S(1)} %bitcast.176, f32[256,1024]{0,1:T(8,128)S(1)} %bitcast.175, f32[256,1024]{0,1:T(8,128)S(1)} %bitcast.174, f32[256,1024]{0,1:T(8,128)S(1)} %bitcast.173, f32[1024]{0:T(1024)S(1)} %copy-done.25, f32[1024,16]{0,1:T(8,128)S(1)} %add_rsqrt_fusion, ...), kind=kLoop, calls=%fused_computation.6 | loop fusion | flops 8388608 | bytes 10620928 | tf_op jit(solution)/shard_map/convert_element_type | solution.py:135
  90.4 3.9 %copy.63 = bf16[1024,1024]{1,0:T(8,128)(2,1)} copy(bf16[1024,1024]{0,1:T(8,128)(2,1)} %fusion.4) | data formatting | bytes 4194304 | tf_op jit(solution)/shard_map/convert_element_type | solution.py:135
  (82 shorter events, 2.3 us)
Async XLA Ops:
  2.4 12.8 %copy-start.21 = (f32[16,256]{1,0:T(8,128)}, f32[16,256]{1,0:T(8,128)S(1)}, u32[]{:S(2)}) copy-start(f32[16,256]{1,0:T(8,128)S(1)} %copy_bitcast_fusion.1) | copy-start | bytes 49156
  2.5 0.6 copy-start.19
  4.8 10.4 %copy-start.23 = (f32[16,256]{1,0:T(8,128)}, f32[16,256]{1,0:T(8,128)S(1)}, u32[]{:S(2)}) copy-start(f32[16,256]{1,0:T(8,128)S(1)} %copy_bitcast_fusion.2) | copy-start | bytes 49156
  5.7 29.6 %collective-permute-start.1 = (f32[16]{0:T(128)}, f32[16]{0:T(128)}, u32[]{:S(2)}, u32[]{:S(2)}) collective-permute-start(f32[16]{0:T(128)} %get-tuple-element.46), channel_id=1, source_target_pairs={{0,4},{4,0},{8,12},{12,8},{16,20},{20,16},{24,28},{28,24},{1,5},{5... | collective-permute-start | bytes 200 | tf_op jit(solution)/shard_map/ppermute | solution.py:12
  15.2 8.7 %copy-start.3 = (bf16[1024,128]{1,0:T(8,128)(2,1)S(1)}, bf16[1024,128]{1,0:T(8,128)(2,1)}, u32[]{:S(2)}) copy-start(bf16[1024,128]{1,0:T(8,128)(2,1)} %param.8) | copy-start | bytes 786436
  15.2 8.7 %copy-start.6 = (bf16[1024,128]{1,0:T(8,128)(2,1)S(1)}, bf16[1024,128]{1,0:T(8,128)(2,1)}, u32[]{:S(2)}) copy-start(bf16[1024,128]{1,0:T(8,128)(2,1)} %param.7) | copy-start | bytes 786436
  15.4 10.3 %copy-start.4 = (bf16[256,1024]{0,1:T(8,128)(2,1)}, bf16[256,1024]{0,1:T(8,128)(2,1)S(1)}, u32[]{:S(2)}) copy-start(bf16[256,1024]{0,1:T(8,128)(2,1)S(1)} %copy.62) | copy-start | bytes 1572868
  19.1 4.7 %copy-start.1 = (f32[16,128,64]{1,2,0:T(8,128)}, f32[16,128,64]{1,2,0:T(8,128)S(1)}, u32[]{:S(2)}) copy-start(f32[16,128,64]{1,2,0:T(8,128)S(1)} %convolution_add_fusion.2) | copy-start | bytes 1572868
  20.7 0.8 copy-start
  23.8 4.9 %copy-start.24 = (f32[16,256]{1,0:T(8,128)S(1)}, f32[16,256]{1,0:T(8,128)}, u32[]{:S(2)}) copy-start(f32[16,256]{1,0:T(8,128)} %copy-done.23) | copy-start | bytes 49156
  23.8 13.7 %collective-permute-start = (f32[16,64,128]{2,1,0:T(8,128)}, f32[16,64,128]{2,1,0:T(8,128)}, u32[]{:S(2)}, u32[]{:S(2)}) collective-permute-start(f32[16,64,128]{2,1,0:T(8,128)} %fusion.49), channel_id=1, source_target_pairs={{0,4},{4,0},{8,12},{12,8},{16,20},{20,16},{24,28},{28,24},{1,5},{5... | collective-permute-start | bytes 1572872 | tf_op jit(solution)/shard_map/ppermute | solution.py:12
  23.9 5.9 %copy-start.14 = (pred[256,256]{1,0:T(8,128)(4,1)}, pred[256,256]{1,0:T(8,128)(4,1)S(1)}, u32[]{:S(2)}) copy-start(pred[256,256]{1,0:T(8,128)(4,1)S(1)} %iota_compare_fusion) | copy-start | bytes 196612
  26.6 2.1 %copy-start.9 = (f32[256,256]{1,0:T(8,128)S(1)}, f32[256,256]{1,0:T(8,128)}, u32[]{:S(2)}) copy-start(f32[256,256]{1,0:T(8,128)} %fusion.78) | copy-start | bytes 786436
  28.7 1.1 %copy-start.8 = (f32[256,256]{1,0:T(8,128)S(1)}, f32[256,256]{1,0:T(8,128)}, u32[]{:S(2)}) copy-start(f32[256,256]{1,0:T(8,128)} %fusion.74) | copy-start | bytes 786436
  28.7 1.1 %copy-start.22 = (f32[16,256]{1,0:T(8,128)S(1)}, f32[16,256]{1,0:T(8,128)}, u32[]{:S(2)}) copy-start(f32[16,256]{1,0:T(8,128)} %copy-done.21) | copy-start | bytes 49156
  29.8 1.2 %copy-start.10 = (f32[256,16]{0,1:T(8,128)S(1)}, f32[256,16]{0,1:T(8,128)}, u32[]{:S(2)}) copy-start(f32[256,16]{0,1:T(8,128)} %get-tuple-element.30) | copy-start | bytes 49156
  29.8 1.5 %copy-start.12 = (f32[256,16]{0,1:T(8,128)S(1)}, f32[256,16]{0,1:T(8,128)}, u32[]{:S(2)}) copy-start(f32[256,16]{0,1:T(8,128)} %get-tuple-element.32) | copy-start | bytes 49156
  29.9 1.8 %copy-start.2 = (f32[16,128,64]{1,2,0:T(8,128)S(1)}, f32[16,128,64]{1,2,0:T(8,128)}, u32[]{:S(2)}) copy-start(f32[16,128,64]{1,2,0:T(8,128)} %copy-done.1) | copy-start | bytes 1572868
  29.9 1.8 %copy-start.13 = (f32[256,16]{0,1:T(8,128)S(1)}, f32[256,16]{0,1:T(8,128)}, u32[]{:S(2)}) copy-start(f32[256,16]{0,1:T(8,128)} %get-tuple-element.35) | copy-start | bytes 49156
  31.0 2.0 %copy-start.5 = (bf16[256,1024]{0,1:T(8,128)(2,1)S(1)}, bf16[256,1024]{0,1:T(8,128)(2,1)}, u32[]{:S(2)}) copy-start(bf16[256,1024]{0,1:T(8,128)(2,1)} %copy-done.4) | copy-start | bytes 1572868
  31.0 2.0 %copy-start.15 = (pred[256,256]{1,0:T(8,128)(4,1)S(1)}, pred[256,256]{1,0:T(8,128)(4,1)}, u32[]{:S(2)}) copy-start(pred[256,256]{1,0:T(8,128)(4,1)} %copy-done.14) | copy-start | bytes 196612
  31.0 2.0 %copy-start.20 = (f32[16,256]{1,0:T(8,128)S(1)}, f32[16,256]{1,0:T(8,128)}, u32[]{:S(2)}) copy-start(f32[16,256]{1,0:T(8,128)} %copy-done.19) | copy-start | bytes 49156
  33.0 9.4 %copy-start.16 = (f32[16,256]{1,0:T(8,128)S(1)}, f32[16,256]{1,0:T(8,128)}, u32[]{:S(2)}) copy-start(f32[16,256]{1,0:T(8,128)} %get-tuple-element.33) | copy-start | bytes 49156
  33.0 9.4 %copy-start.17 = (f32[16,256]{1,0:T(8,128)S(1)}, f32[16,256]{1,0:T(8,128)}, u32[]{:S(2)}) copy-start(f32[16,256]{1,0:T(8,128)} %get-tuple-element.36) | copy-start | bytes 49156
  33.0 9.4 %copy-start.18 = (f32[16,256]{1,0:T(8,128)S(1)}, f32[16,256]{1,0:T(8,128)}, u32[]{:S(2)}) copy-start(f32[16,256]{1,0:T(8,128)} %get-tuple-element.39) | copy-start | bytes 49156
  33.0 10.4 %copy-start.11 = (f32[256,16]{0,1:T(8,128)S(1)}, f32[256,16]{0,1:T(8,128)}, u32[]{:S(2)}) copy-start(f32[256,16]{0,1:T(8,128)} %get-tuple-element.38) | copy-start | bytes 49156
  40.9 12.8 %collective-permute-start.2 = (f32[16,64,128]{2,1,0:T(8,128)}, f32[16,64,128]{2,1,0:T(8,128)}, u32[]{:S(2)}, u32[]{:S(2)}) collective-permute-start(f32[16,64,128]{2,1,0:T(8,128)} %select_add_fusion.1), channel_id=1, source_target_pairs={{0,8},{4,12},{8,0},{12,4},{16,24},{20,28},{24,16},{28,20},{1,9},{5... | collective-permute-start | bytes 1572872 | tf_op jit(solution)/shard_map/ppermute | solution.py:12
  42.5 16.0 %copy-start.7 = (f32[4,16,1024]{2,1,0:T(8,128)S(1)}, f32[4,16,1024]{2,1,0:T(8,128)}, u32[]{:S(2)}) copy-start(f32[4,16,1024]{2,1,0:T(8,128)} %param.10) | copy-start | bytes 786436
  45.1 8.6 %collective-permute-start.3 = (f32[16]{0:T(128)}, f32[16]{0:T(128)S(1)}, u32[]{:S(2)}, u32[]{:S(2)}) collective-permute-start(f32[16]{0:T(128)} %get-tuple-element.41), channel_id=1, source_target_pairs={{0,8},{4,12},{8,0},{12,4},{16,24},{20,28},{24,16},{28,20},{1,9},{5... | collective-permute-start | bytes 200 | tf_op jit(solution)/shard_map/ppermute | solution.py:12
  55.7 23.7 %collective-permute-start.4 = (f32[16,64,128]{2,1,0:T(8,128)S(1)}, f32[16,64,128]{2,1,0:T(8,128)S(1)}, u32[]{:S(2)}, u32[]{:S(2)}) collective-permute-start(f32[16,64,128]{2,1,0:T(8,128)S(1)} %select_add_fusion), channel_id=1, source_target_pairs={{0,16},{4,20},{8,24},{12,28},{16,0},{20,4},{24,8},{28,12},{1,17},{... | collective-permute-start | bytes 1572872 | tf_op jit(solution)/shard_map/ppermute | solution.py:12
  87.1 1.0 %copy-start.25 = (f32[1024]{0:T(1024)S(1)}, f32[1024]{0:T(1024)}, u32[]{:S(2)}) copy-start(f32[1024]{0:T(1024)} %param.11) | copy-start | bytes 12292
where the time goes:
time: 95 us; the launch traced here: 94.3 us
  waiting for transfers between devices  31.2 us (33%)
  matrix products  27.8 us (29%)
  other arithmetic  16.9 us (18%)
  local copies, waits for them, and re-layouts  10.3 us (11%)
  starting transfers between devices  7.72 us (8%)
    ppermute x5, waiting for transfers between devices, partner_2(): lax.ppermute(array, axis, [(i, i ^ 1 << bit) for i in range(lax.axis_size...  31.2 us
    ppermute x5, starting transfers between devices, partner_2(): lax.ppermute(array, axis, [(i, i ^ 1 << bit) for i in range(lax.axis_size...  7.72 us
    dot_general x1, matrix products, far_terms(): jnp.einsum('tn,lkn->ltk', out_rows.astype(jnp.float32), stacked.reshape(l...  7.7 us
    dot_general x4, matrix products, piece_scan(): jnp.einsum('shp,hsn->hpn', val_piece, weighted, preferred_element_type=jn...  7.35 us
    dot_general x4, matrix products, piece_scan(): jnp.einsum('hts,shp->thp', mixing, val_piece, preferred_element_type=jnp....  6.44 us
    convert_element_type x1, local copies, waits for them, and re-layouts, per_device(): return (combined * scale_wide * norm_gain[None, :]).astype(jnp.bfloat16)  3.93 us
    dot_general x4, matrix products, piece_scan(): scores = jnp.dot(out_piece, in_piece.T, preferred_element_type=jnp.float32)  3.71 us
    add x2, other arithmetic, merge_pair(): jnp.exp(upper_side[1])[:, None, None] * lower_side[0] + upper_side[0]  3.45 us
  transfers between devices with their start and end apart: 5, of which 3 were waited for; matrix products, arithmetic and copies ran while one was open for 30% of the time, Pallas kernels for 0%

commit v1 on v0

v1 whole, which is shorter than its diff:
```python
import functools

import jax
import jax.numpy as jnp
from jax import lax
from jax.experimental import pallas as pl
from jax.experimental.pallas import tpu as pltpu
from jax.sharding import PartitionSpec as P

P_SIZE = 64
N = 128
STEP = 128
LANES = 256
FAR_ROWS = 256
F32 = jnp.float32
BF16 = jnp.bfloat16
MESH = pl.DeviceIdType.MESH
EXACT = lax.Precision.HIGHEST


def dot(a, b, precision=None):
    return jnp.dot(a, b, preferred_element_type=F32, precision=precision)


def split_two(x):
    high = x.astype(BF16)
    return high, (x - high.astype(F32)).astype(BF16)


def kernel(
    n_outer,
    n_inner,
    v_ref,
    b_ref,
    c_ref,
    d_ref,
    g_ref,
    gain_ref,
    o_ref,
    w_ref,
    e_ref,
    bt_ref,
    x_ref,
    r_ref,
    rows_ref,
    gap_ref,
    acc_ref,
    agg_ref,
    got_ref,
    send_sem,
    pass_sem,
    recv_sem,
):
    tokens, width = v_ref.shape
    heads = d_ref.shape[0]
    steps = tokens // STEP
    chunks = width // LANES
    inner_bits = n_inner.bit_length() - 1
    outer_bits = n_outer.bit_length() - 1
    bits = inner_bits + outer_bits
    outer = lax.axis_index("outer")
    inner = lax.axis_index("inner")

    def bit_of(number, bit):
        return lax.rem(number // (1 << bit), 2)

    def flipped(bit):
        return inner + (1 - 2 * bit_of(inner, bit)) * (1 << bit)

    barrier = pltpu.get_barrier_semaphore()
    for bit in range(inner_bits):
        pl.semaphore_signal(barrier, inc=1, device_id={"inner": flipped(bit)}, device_id_type=MESH)

    @pl.when(outer > 0)
    def _():
        pl.semaphore_signal(barrier, inc=1, device_id={"outer": outer - 1}, device_id_type=MESH)

    @pl.when(outer < n_outer - 1)
    def _():
        pl.semaphore_signal(barrier, inc=1, device_id={"outer": outer + 1}, device_id_type=MESH)

    row_i = lax.broadcasted_iota(jnp.int32, (STEP, STEP), 0)
    col_i = lax.broadcasted_iota(jnp.int32, (STEP, STEP), 1)
    upto = (row_i <= col_i).astype(F32)
    spread_f = (
        lax.broadcasted_iota(jnp.int32, (heads, width), 1) // P_SIZE
        == lax.broadcasted_iota(jnp.int32, (heads, width), 0)
    ).astype(F32)
    e_ref[...] = jnp.concatenate([spread_f, spread_f], axis=0).astype(BF16)
    stacked = jnp.concatenate(
        [d_ref[:, c * STEP : (c + 1) * STEP] for c in range(steps)], axis=0
    )
    run_all = dot(stacked, upto, EXACT)
    offset = jnp.zeros((heads, 1), F32)
    last_columns = []
    for c in range(steps):
        span = slice(c * STEP, (c + 1) * STEP)
        run = run_all[c * heads : (c + 1) * heads]
        last = run[:, STEP - 1 : STEP]
        last_columns.append(last)
        centre = 0.5 * last
        grown = jnp.exp(run - centre)
        cum_exp = jnp.exp(run + offset)
        kinds = [jnp.exp(centre - run), g_ref[0, :, span] * grown]
        for bit in range(bits):
            kinds.append(g_ref[bit + 1, :, span] * cum_exp)
        for kind, weight in enumerate(kinds):
            high = weight.astype(BF16).astype(F32)
            both = jnp.concatenate([high, weight - high], axis=0)
            w_ref[kind, span, :] = both.T.astype(BF16)
        offset = offset + last
        bt_ref[c] = b_ref[span, :].astype(F32).T.astype(BF16)
        scores = lax.dot_general(
            c_ref[span, :],
            b_ref[span, :],
            (((1,), (1,)), ((), ())),
            preferred_element_type=F32,
        )
        x_ref[span, 0:STEP] = jnp.where(row_i >= col_i, scores, 0.0).astype(BF16)
        x_ref[span, STEP:] = c_ref[span, :]
    step_logs = jnp.concatenate(
        [jnp.broadcast_to(last, (heads, STEP)) for last in last_columns], axis=0
    )
    for c in range(steps):
        one = step_logs[c * heads : (c + 1) * heads].T[0:8]
        rows_ref[c] = dot(one, spread_f, EXACT)

    def lanes(q):
        return slice(q * LANES, (q + 1) * LANES)

    def weight_of(kind, rows, q):
        return dot(w_ref[kind, rows, :], e_ref[:, lanes(q)])

    def copy_to(source, level, q, sem, device):
        return pltpu.make_async_remote_copy(
            src_ref=source,
            dst_ref=got_ref.at[level, q],
            send_sem=sem.at[level, q],
            recv_sem=recv_sem.at[level, q],
            device_id=device,
            device_id_type=MESH,
        )

    def halved(level):
        return inner_bits > 0 and level > inner_bits

    def mine(q):
        return lax.rem(inner, 2) == q % 2

    def outer_sends(level, q, action):
        bit = level - inner_bits
        goes = jnp.logical_and(outer < n_outer - 1, bit_of(outer + 1, bit) == 1)
        if halved(level):
            goes = jnp.logical_and(goes, mine(q))
        return goes, bit

    def start_outer(level, q, from_agg):
        goes, bit = outer_sends(level, q, None)
        kind = bit_of(outer, bit) == (0 if from_agg else 1)
        source = agg_ref.at[level, q] if from_agg else got_ref.at[level, q]

        @pl.when(jnp.logical_and(goes, kind))
        def _():
            copy_to(source, level, q, send_sem, {"outer": outer + 1}).start()

    def start_level(level, q):
        if level >= bits:
            return
        if level < inner_bits:
            copy_to(
                agg_ref.at[level, q], level, q, send_sem, {"inner": flipped(level)}
            ).start()
        else:
            start_outer(level, q, True)

    def near(q):
        state = jnp.zeros((N, LANES), F32)
        total = jnp.zeros((8, LANES), F32)
        for c in range(steps):
            span = slice(c * STEP, (c + 1) * STEP)
            scaled = (v_ref[span, lanes(q)].astype(F32) * weight_of(0, span, q)).astype(BF16)
            log_rows = rows_ref[c, :, lanes(q)]
            factor = jnp.exp(0.5 * log_rows[0:1])
            shrunk = factor * state
            r_ref[c, 0:STEP, lanes(q)] = scaled
            r_ref[c, STEP:, lanes(q)] = shrunk.astype(BF16)
            state = factor * (shrunk + dot(bt_ref[c], scaled))
            total = total + log_rows
        agg_ref[0, q, 0:N] = state
        agg_ref[0, q, N:] = total
        gap_ref[q] = jnp.zeros((8, LANES), F32)

    def local(q):
        for c in range(steps):
            span = slice(c * STEP, (c + 1) * STEP)
            acc_ref[span, lanes(q)] = dot(x_ref[span, :], r_ref[c, :, lanes(q)]) * weight_of(
                1, span, q
            )

    def far(level, q):
        gap = gap_ref[q]
        bucket = got_ref[level, q, 0:N] * jnp.exp(gap[0:1])
        gap_ref[q] = gap + got_ref[level, q, N:]
        high, low = split_two(bucket)
        right = jnp.concatenate([high, low], axis=0)
        for t in range(tokens // FAR_ROWS):
            span = slice(t * FAR_ROWS, (t + 1) * FAR_ROWS)
            left = x_ref[span, STEP:]
            product = dot(jnp.concatenate([left, left], axis=1), right)
            acc_ref[span, lanes(q)] += product * weight_of(2 + level, span, q)

    def merge(level, q, lower, upper):
        upper_log = upper[N:]
        agg_ref[level + 1, q, 0:N] = jnp.exp(upper_log[0:1]) * lower[0:N] + upper[0:N]
        agg_ref[level + 1, q, N:] = lower[N:] + upper_log

    def wait_got(level, q):
        copy_to(got_ref.at[level, q], level, q, send_sem, {"inner": inner}).wait_recv()

    def handle(level, q):
        if level < inner_bits:
            wait_got(level, q)
            upper = bit_of(inner, level) == 1
            if level + 1 < bits:

                @pl.when(upper)
                def _():
                    merge(level, q, got_ref.at[level, q], agg_ref.at[level, q])

                @pl.when(jnp.logical_not(upper))
                def _():
                    merge(level, q, agg_ref.at[level, q], got_ref.at[level, q])

                start_level(level + 1, q)
            pl.when(upper)(lambda: far(level, q))
            return
        bit = level - inner_bits

        @pl.when(bit_of(outer, bit) == 1)
        def _():
            wait_got(level, q)
            start_outer(level, q, False)
            if halved(level):

                @pl.when(mine(q))
                def _():
                    copy_to(
                        got_ref.at[level, q], level, q, pass_sem, {"inner": flipped(0)}
                    ).start()

            if level + 1 < bits:
                merge(level, q, got_ref.at[level, q], agg_ref.at[level, q])
                start_level(level + 1, q)
            far(level, q)

    averaging = (
        lax.broadcasted_iota(jnp.int32, (LANES, LANES), 0) // P_SIZE
        == lax.broadcasted_iota(jnp.int32, (LANES, LANES), 1) // P_SIZE
    )
    averaging = jnp.where(averaging, 1.0 / P_SIZE, 0.0).astype(BF16)

    def finish(q):
        gain = gain_ref[:, lanes(q)]
        for t in range(tokens // FAR_ROWS):
            span = slice(t * FAR_ROWS, (t + 1) * FAR_ROWS)
            combined = acc_ref[span, lanes(q)]
            mean_square = dot((combined * combined).astype(BF16), averaging)
            o_ref[span, lanes(q)] = (
                combined * lax.rsqrt(mean_square + 1e-05) * gain
            ).astype(BF16)

    for q in range(chunks):
        near(q)
        if q == 0:
            below = (outer + n_outer - 1) // n_outer
            above = 1 - (outer + 1) // n_outer
            pl.semaphore_wait(barrier, inner_bits + below + above)
        start_level(0, q)
    for tick in range(chunks + bits - 1):
        if tick < chunks:
            local(tick)
        for level in range(bits):
            q = tick - level
            if 0 <= q < chunks:
                handle(level, q)
                if level == bits - 1:
                    finish(q)
    for level in range(bits):
        for q in range(chunks):
            if level < inner_bits:
                copy_to(
                    agg_ref.at[level, q], level, q, send_sem, {"inner": flipped(level)}
                ).wait_send()
                continue
            goes, bit = outer_sends(level, q, None)

            @pl.when(goes)
            def _():
                copy_to(
                    agg_ref.at[level, q], level, q, send_sem, {"inner": inner}
                ).wait_send()

            if halved(level):

                @pl.when(jnp.logical_and(bit_of(outer, bit) == 1, mine(q)))
                def _():
                    copy_to(
                        got_ref.at[level, q], level, q, pass_sem, {"inner": flipped(0)}
                    ).wait_send()


def per_device(n_outer, n_inner, values, input_state, output_state, decay, gates, gain):
    tokens, width = values.shape
    heads = decay.shape[0]
    bits = n_outer.bit_length() + n_inner.bit_length() - 2
    steps, chunks = tokens // STEP, width // LANES
    flight = (bits, chunks, N + 8, LANES)
    in_vmem = pl.BlockSpec(memory_space=pltpu.VMEM)
    return pl.pallas_call(
        functools.partial(kernel, n_outer, n_inner),
        out_shape=jax.ShapeDtypeStruct((tokens, width), BF16),
        in_specs=[in_vmem] * 6,
        out_specs=in_vmem,
        scratch_shapes=[
            pltpu.VMEM((2 + bits, tokens, 2 * heads), BF16),
            pltpu.VMEM((2 * heads, width), BF16),
            pltpu.VMEM((steps, N, STEP), BF16),
            pltpu.VMEM((tokens, STEP + N), BF16),
            pltpu.VMEM((steps, STEP + N, width), BF16),
            pltpu.VMEM((steps, 8, width), F32),
            pltpu.VMEM((chunks, 8, LANES), F32),
            pltpu.VMEM((tokens, width), F32),
            pltpu.VMEM(flight, F32),
            pltpu.VMEM(flight, F32),
            pltpu.SemaphoreType.DMA((bits, chunks)),
            pltpu.SemaphoreType.DMA((bits, chunks)),
            pltpu.SemaphoreType.DMA((bits, chunks)),
        ],
        compiler_params=pltpu.CompilerParams(
            collective_id=0, has_side_effects=True, vmem_limit_bytes=56 * 1024 * 1024
        ),
    )(values, input_state, output_state, decay, gates, gain.reshape(1, width))


def solution(mesh):
    sequence = ("outer", "inner")
    return jax.shard_map(
        functools.partial(per_device, mesh.shape["outer"], mesh.shape["inner"]),
        mesh=mesh,
        in_specs=(
            P(sequence, "head"),
            P(sequence, None),
            P(sequence, None),
            P("head", sequence),
            P(None, "head", sequence),
            P("head"),
        ),
        out_specs=P(sequence, "head"),
        check_vma=False,
    )
```

time: 95 us -> 49.3 us (0.52)
  the two profiles are of different devices: /device:TPU:0 before, /device:TPU:26 now
where the time goes in v1:
time: 49.3 us; the launch traced here: 49.1 us
  Pallas kernels  46 us (93%)
  local copies, waits for them, and re-layouts  3.08 us (6%)
    pallas_call x1, Pallas kernels, per_device(): pl.pallas_call(functools.partial(kernel, n_outer, n_inner), out_shape=jax...  46 us
    unnamed x1, local copies, waits for them, and re-layouts  3.08 us

profile of v1, /device:TPU:26, one launch (start us, length us, event | category | flops | bytes accessed | tf_op | source)
XLA Modules:
  0.0 49.1 jit_solution(17774690198894523182)
XLA Ops:
  0.0 46.0 %shard_map.64 = bf16[1024,1024]{1,0:T(8,128)(2,1)} custom-call(bf16[1024,1024]{1,0:T(8,128)(2,1)} %v_ref.1, bf16[1024,128]{1,0:T(8,128)(2,1)} %b_ref.1, bf16[1024,128]{1,0:T(8,128)(2,1)} %c_ref.1, f32[16,1024]{1,0:T(8,128)} %d_ref.1, f32[4,16,1024]{2,1,0:T(8,128)} %g_ref.1, f32[1,1024]{1,0:T(1,128)} %bitcast.1), custom_call_target="tpu_custom_call" | custom-call | tf_op jit(solution)/shard_map/pallas_call | solution.py:319
  46.1 3.1 %copy.8 = bf16[1024,1024]{1,0:T(8,128)(2,1)} copy(bf16[1024,1024]{1,0:T(8,128)(2,1)} %shard_map.64) | data formatting | bytes 4194304

commit v2 on v1

--- a/solution.py
+++ b/solution.py
@@ -11,6 +11,7 @@
 N = 128
 STEP = 128
 LANES = 256
+UNIT = 128
 FAR_ROWS = 256
 F32 = jnp.float32
 BF16 = jnp.bfloat16
@@ -131,12 +132,19 @@
     def weight_of(kind, rows, q):
         return dot(w_ref[kind, rows, :], e_ref[:, lanes(q)])
 
-    def copy_to(source, level, q, sem, device):
+    parity = lax.rem(inner, 2)
+    own_parity = (parity, 1 - parity)
+    top_row = outer == n_outer - 1
+
+    def unit_of(q, late):
+        return 2 * q + own_parity[late]
+
+    def copy_to(source, level, u, sem, device):
         return pltpu.make_async_remote_copy(
             src_ref=source,
-            dst_ref=got_ref.at[level, q],
-            send_sem=sem.at[level, q],
-            recv_sem=recv_sem.at[level, q],
+            dst_ref=got_ref.at[level, u],
+            send_sem=sem.at[level, u],
+            recv_sem=recv_sem.at[level, u],
             device_id=device,
             device_id_type=MESH,
         )
@@ -144,34 +152,126 @@
     def halved(level):
         return inner_bits > 0 and level > inner_bits
 
-    def mine(q):
-        return lax.rem(inner, 2) == q % 2
-
-    def outer_sends(level, q, action):
+    def skips(level, upper):
+        return jnp.logical_and(top_row, upper) if level == inner_bits - 1 else None
+
+    def unless(skip, action):
+        if skip is None:
+            action()
+        else:
+            pl.when(jnp.logical_not(skip))(action)
+
+    def goes_up(level):
         bit = level - inner_bits
-        goes = jnp.logical_and(outer < n_outer - 1, bit_of(outer + 1, bit) == 1)
+        return jnp.logical_and(outer < n_outer - 1, bit_of(outer + 1, bit) == 1)
+
+    def own_up(level):
+        return jnp.logical_and(goes_up(level), bit_of(outer, level - inner_bits) == 0)
+
+    def pass_up(level):
+        return jnp.logical_and(goes_up(level), bit_of(outer, level - inner_bits) == 1)
+
+    def inner_copy(level, u):
+        return copy_to(agg_ref.at[level, u], level, u, send_sem, {"inner": flipped(level)})
+
+    def up_copy(source, level, u):
+        return copy_to(source, level, u, send_sem, {"outer": outer + 1})
+
+    def swap_copy(level, u):
+        return copy_to(got_ref.at[level, u], level, u, pass_sem, {"inner": flipped(0)})
+
+    def start_first(q, late):
+        if inner_bits:
+            u = unit_of(q, 1 - late)
+            unless(skips(0, bit_of(inner, 0) == 1), lambda: inner_copy(0, u).start())
+        else:
+            u = unit_of(q, late)
+            pl.when(own_up(0))(lambda: up_copy(agg_ref.at[0, u], 0, u).start())
+
+    def merge(level, u, lower, upper):
+        upper_log = upper[N:]
+        agg_ref[level + 1, u, 0:N] = jnp.exp(upper_log[0:1]) * lower[0:N] + upper[0:N]
+        agg_ref[level + 1, u, N:] = lower[N:] + upper_log
+
+    def handle(level, q, late):
+        u = unit_of(q, late)
+        got, held = got_ref.at[level, u], agg_ref.at[level, u]
+        if level < inner_bits:
+            upper = bit_of(inner, level) == 1
+
+            def take():
+                inner_copy(level, u).wait_recv()
+                following = level + 1
+                if following == bits or (late and halved(following)):
+                    return
+
+                def join():
+                    pl.when(upper)(lambda: merge(level, u, got, held))
+                    pl.when(jnp.logical_not(upper))(lambda: merge(level, u, held, got))
+
+                if following < inner_bits:
+                    join()
+                    unless(
+                        skips(following, bit_of(inner, following) == 1),
+                        lambda: inner_copy(following, u).start(),
+                    )
+                    return
+
+                @pl.when(outer < n_outer - 1)
+                def _():
+                    join()
+
+                @pl.when(own_up(following))
+                def _():
+                    up_copy(agg_ref.at[following, u], following, u).start()
+
+            unless(skips(level, jnp.logical_not(upper)), take)
+            return
+
+        @pl.when(bit_of(outer, level - inner_bits) == 1)
+        def _():
+            up_copy(held, level, u).wait_recv()
+            if late and halved(level):
+                return
+
+            @pl.when(pass_up(level))
+            def _():
+                up_copy(got, level, u).start()
+
+            if halved(level):
+                swap_copy(level, u).start()
+            following = level + 1
+            if following == bits or (late and halved(following)):
+                return
+
+            @pl.when(outer < n_outer - 1)
+            def _():
+                merge(level, u, got, held)
+
+            @pl.when(own_up(following))
+            def _():
+                up_copy(agg_ref.at[following, u], following, u).start()
+
+    def wait_sent(level, q, late):
+        u = unit_of(q, late)
+        if level < inner_bits:
+            unless(
+                skips(level, bit_of(inner, level) == 1),
+                lambda: inner_copy(level, u).wait_send(),
+            )
+            return
+        if late and halved(level):
+            return
+        pl.when(goes_up(level))(lambda: up_copy(agg_ref.at[level, u], level, u).wait_send())
         if halved(level):
-            goes = jnp.logical_and(goes, mine(q))
-        return goes, bit
-
-    def start_outer(level, q, from_agg):
-        goes, bit = outer_sends(level, q, None)
-        kind = bit_of(outer, bit) == (0 if from_agg else 1)
-        source = agg_ref.at[level, q] if from_agg else got_ref.at[level, q]
-
-        @pl.when(jnp.logical_and(goes, kind))
-        def _():
-            copy_to(source, level, q, send_sem, {"outer": outer + 1}).start()
-
-    def start_level(level, q):
-        if level >= bits:
-            return
+            pl.when(bit_of(outer, level - inner_bits) == 1)(
+                lambda: swap_copy(level, u).wait_send()
+            )
+
+    def needs(level):
         if level < inner_bits:
-            copy_to(
-                agg_ref.at[level, q], level, q, send_sem, {"inner": flipped(level)}
-            ).start()
-        else:
-            start_outer(level, q, True)
+            return bit_of(inner, level) == 1
+        return bit_of(outer, level - inner_bits) == 1
 
     def near(q):
         state = jnp.zeros((N, LANES), F32)
@@ -186,8 +286,10 @@
             r_ref[c, STEP:, lanes(q)] = shrunk.astype(BF16)
             state = factor * (shrunk + dot(bt_ref[c], scaled))
             total = total + log_rows
-        agg_ref[0, q, 0:N] = state
-        agg_ref[0, q, N:] = total
+        for side in range(2):
+            half = slice(side * UNIT, (side + 1) * UNIT)
+            agg_ref[0, 2 * q + side, 0:N] = state[:, half]
+            agg_ref[0, 2 * q + side, N:] = total[:, half]
         gap_ref[q] = jnp.zeros((8, LANES), F32)
 
     def local(q):
@@ -199,8 +301,9 @@
 
     def far(level, q):
         gap = gap_ref[q]
-        bucket = got_ref[level, q, 0:N] * jnp.exp(gap[0:1])
-        gap_ref[q] = gap + got_ref[level, q, N:]
+        arrived = jnp.concatenate([got_ref[level, 2 * q], got_ref[level, 2 * q + 1]], axis=1)
+        bucket = arrived[0:N] * jnp.exp(gap[0:1])
+        gap_ref[q] = gap + arrived[N:]
         high, low = split_two(bucket)
         right = jnp.concatenate([high, low], axis=0)
         for t in range(tokens // FAR_ROWS):
@@ -208,50 +311,6 @@
             left = x_ref[span, STEP:]
             product = dot(jnp.concatenate([left, left], axis=1), right)
             acc_ref[span, lanes(q)] += product * weight_of(2 + level, span, q)
-
-    def merge(level, q, lower, upper):
-        upper_log = upper[N:]
-        agg_ref[level + 1, q, 0:N] = jnp.exp(upper_log[0:1]) * lower[0:N] + upper[0:N]
-        agg_ref[level + 1, q, N:] = lower[N:] + upper_log
-
-    def wait_got(level, q):
-        copy_to(got_ref.at[level, q], level, q, send_sem, {"inner": inner}).wait_recv()
-
-    def handle(level, q):
-        if level < inner_bits:
-            wait_got(level, q)
-            upper = bit_of(inner, level) == 1
-            if level + 1 < bits:
-
-                @pl.when(upper)
-                def _():
-                    merge(level, q, got_ref.at[level, q], agg_ref.at[level, q])
-
-                @pl.when(jnp.logical_not(upper))
-                def _():
-                    merge(level, q, agg_ref.at[level, q], got_ref.at[level, q])
-
-                start_level(level + 1, q)
-            pl.when(upper)(lambda: far(level, q))
-            return
-        bit = level - inner_bits
-
-        @pl.when(bit_of(outer, bit) == 1)
-        def _():
-            wait_got(level, q)
-            start_outer(level, q, False)
-            if halved(level):
-
-                @pl.when(mine(q))
-                def _():
-                    copy_to(
-                        got_ref.at[level, q], level, q, pass_sem, {"inner": flipped(0)}
-                    ).start()
-
-            if level + 1 < bits:
-                merge(level, q, got_ref.at[level, q], agg_ref.at[level, q])
-                start_level(level + 1, q)
-            far(level, q)
 
     averaging = (
         lax.broadcasted_iota(jnp.int32, (LANES, LANES), 0) // P_SIZE
@@ -275,38 +334,28 @@
             below = (outer + n_outer - 1) // n_outer
             above = 1 - (outer + 1) // n_outer
             pl.semaphore_wait(barrier, inner_bits + below + above)
-        start_level(0, q)
-    for tick in range(chunks + bits - 1):
-        if tick < chunks:
-            local(tick)
-        for level in range(bits):
-            q = tick - level
-            if 0 <= q < chunks:
-                handle(level, q)
-                if level == bits - 1:
-                    finish(q)
+        start_first(q, 0)
+    for q in range(chunks):
+        start_first(q, 1)
+    events = []
     for level in range(bits):
-        for q in range(chunks):
-            if level < inner_bits:
-                copy_to(
-                    agg_ref.at[level, q], level, q, send_sem, {"inner": flipped(level)}
-                ).wait_send()
-                continue
-            goes, bit = outer_sends(level, q, None)
-
-            @pl.when(goes)
-            def _():
-                copy_to(
-                    agg_ref.at[level, q], level, q, send_sem, {"inner": inner}
-                ).wait_send()
-
-            if halved(level):
-
-                @pl.when(jnp.logical_and(bit_of(outer, bit) == 1, mine(q)))
-                def _():
-                    copy_to(
-                        got_ref.at[level, q], level, q, pass_sem, {"inner": flipped(0)}
-                    ).wait_send()
+        for late in range(2):
+            for q in range(chunks):
+                due = q + late * (chunks + 0.5) + 1.6 * level
+                events.append((due, level, q, late))
+    events.sort()
+    for at, (_, level, q, late) in enumerate(events):
+        handle(level, q, late)
+        if at < chunks:
+            local(at)
+        if late:
+            pl.when(needs(level))(lambda: far(level, q))
+            if level == bits - 1:
+                finish(q)
+    for level in range(bits):
+        for late in range(2):
+            for q in range(chunks):
+                wait_sent(level, q, late)
 
 
 def per_device(n_outer, n_inner, values, input_state, output_state, decay, gates, gain):
@@ -314,7 +363,8 @@
     heads = decay.shape[0]
     bits = n_outer.bit_length() + n_inner.bit_length() - 2
     steps, chunks = tokens // STEP, width // LANES
-    flight = (bits, chunks, N + 8, LANES)
+    units = width // UNIT
+    flight = (bits, units, N + 8, UNIT)
     in_vmem = pl.BlockSpec(memory_space=pltpu.VMEM)
     return pl.pallas_call(
         functools.partial(kernel, n_outer, n_inner),
@@ -332,9 +382,9 @@
             pltpu.VMEM((tokens, width), F32),
             pltpu.VMEM(flight, F32),
             pltpu.VMEM(flight, F32),
-            pltpu.SemaphoreType.DMA((bits, chunks)),
-            pltpu.SemaphoreType.DMA((bits, chunks)),
-            pltpu.SemaphoreType.DMA((bits, chunks)),
+            pltpu.SemaphoreType.DMA((bits, units)),
+            pltpu.SemaphoreType.DMA((bits, units)),
+            pltpu.SemaphoreType.DMA((bits, units)),
         ],
         compiler_params=pltpu.CompilerParams(
             collective_id=0, has_side_effects=True, vmem_limit_bytes=56 * 1024 * 1024

time: 49.3 us -> 34.6 us (0.70)
  Pallas kernels: 46 us -> 31.3 us
    pallas_call x1, Pallas kernels: 46 us -> 31.3 us  [per_device(): pl.pallas_call(functools.partial(kernel, n_outer, n_inner), out_shape=jax...]
where the time goes in v2:
time: 34.6 us; the launch traced here: 34.4 us
  Pallas kernels  31.3 us (90%)
  local copies, waits for them, and re-layouts  3.08 us (9%)
    pallas_call x1, Pallas kernels, per_device(): pl.pallas_call(functools.partial(kernel, n_outer, n_inner), out_shape=jax...  31.3 us
    unnamed x1, local copies, waits for them, and re-layouts  3.08 us

profile of v2, /device:TPU:26, one launch (start us, length us, event | category | flops | bytes accessed | tf_op | source)
XLA Modules:
  0.0 34.4 jit_solution(16640700960723529003)
XLA Ops:
  0.0 31.3 %shard_map.64 = bf16[1024,1024]{1,0:T(8,128)(2,1)} custom-call(bf16[1024,1024]{1,0:T(8,128)(2,1)} %v_ref.1, bf16[1024,128]{1,0:T(8,128)(2,1)} %b_ref.1, bf16[1024,128]{1,0:T(8,128)(2,1)} %c_ref.1, f32[16,1024]{1,0:T(8,128)} %d_ref.1, f32[4,16,1024]{2,1,0:T(8,128)} %g_ref.1, f32[1,1024]{1,0:T(1,128)} %bitcast.1), custom_call_target="tpu_custom_call" | custom-call | tf_op jit(solution)/shard_map/pallas_call | solution.py:369
  31.3 3.1 %copy.8 = bf16[1024,1024]{1,0:T(8,128)(2,1)} copy(bf16[1024,1024]{1,0:T(8,128)(2,1)} %shard_map.64) | data formatting | bytes 4194304

commit v3 on v2

--- a/solution.py
+++ b/solution.py
@@ -31,12 +31,19 @@
 def kernel(
     n_outer,
     n_inner,
+    v_hbm,
+    b_hbm,
+    c_hbm,
+    d_hbm,
+    g_hbm,
+    gain_hbm,
+    o_hbm,
     v_ref,
     b_ref,
+    d_ref,
+    gain_ref,
     c_ref,
-    d_ref,
     g_ref,
-    gain_ref,
     o_ref,
     w_ref,
     e_ref,
@@ -51,9 +58,11 @@
     send_sem,
     pass_sem,
     recv_sem,
+    in_sem,
+    out_sem,
 ):
-    tokens, width = v_ref.shape
-    heads = d_ref.shape[0]
+    tokens, width = v_hbm.shape
+    heads = d_hbm.shape[0]
     steps = tokens // STEP
     chunks = width // LANES
     inner_bits = n_inner.bit_length() - 1
@@ -61,6 +70,19 @@
     bits = inner_bits + outer_bits
     outer = lax.axis_index("outer")
     inner = lax.axis_index("inner")
+    v_copies = [
+        pltpu.make_async_copy(v_hbm.at[:, span], v_ref.at[:, span], in_sem.at[q])
+        for q, span in enumerate(
+            pl.ds(first, LANES) for first in range(0, width, LANES)
+        )
+    ]
+    g_copy = pltpu.make_async_copy(g_hbm, g_ref, in_sem.at[chunks])
+    c_copy = pltpu.make_async_copy(c_hbm, c_ref, in_sem.at[chunks + 1])
+    d_copy = pltpu.make_async_copy(d_hbm, d_ref, in_sem.at[chunks + 2])
+    b_copy = pltpu.make_async_copy(b_hbm, b_ref, in_sem.at[chunks + 3])
+    gain_copy = pltpu.make_async_copy(gain_hbm, gain_ref, in_sem.at[chunks + 4])
+    for copy in [d_copy, b_copy] + v_copies + [g_copy, c_copy, gain_copy]:
+        copy.start()
 
     def bit_of(number, bit):
         return lax.rem(number // (1 << bit), 2)
@@ -88,37 +110,51 @@
         == lax.broadcasted_iota(jnp.int32, (heads, width), 0)
     ).astype(F32)
     e_ref[...] = jnp.concatenate([spread_f, spread_f], axis=0).astype(BF16)
+    d_copy.wait()
+    b_copy.wait()
     stacked = jnp.concatenate(
         [d_ref[:, c * STEP : (c + 1) * STEP] for c in range(steps)], axis=0
     )
     run_all = dot(stacked, upto, EXACT)
-    offset = jnp.zeros((heads, 1), F32)
+    def put_weight(kind, span, weight):
+        high = weight.astype(BF16).astype(F32)
+        both = jnp.concatenate([high, weight - high], axis=0)
+        w_ref[kind, span, :] = both.T.astype(BF16)
+
+    def run_of(c):
+        return run_all[c * heads : (c + 1) * heads]
+
     last_columns = []
     for c in range(steps):
         span = slice(c * STEP, (c + 1) * STEP)
-        run = run_all[c * heads : (c + 1) * heads]
+        run = run_of(c)
         last = run[:, STEP - 1 : STEP]
         last_columns.append(last)
-        centre = 0.5 * last
-        grown = jnp.exp(run - centre)
-        cum_exp = jnp.exp(run + offset)
-        kinds = [jnp.exp(centre - run), g_ref[0, :, span] * grown]
-        for bit in range(bits):
-            kinds.append(g_ref[bit + 1, :, span] * cum_exp)
-        for kind, weight in enumerate(kinds):
-            high = weight.astype(BF16).astype(F32)
-            both = jnp.concatenate([high, weight - high], axis=0)
-            w_ref[kind, span, :] = both.T.astype(BF16)
-        offset = offset + last
+        put_weight(0, span, jnp.exp(0.5 * last - run))
         bt_ref[c] = b_ref[span, :].astype(F32).T.astype(BF16)
-        scores = lax.dot_general(
-            c_ref[span, :],
-            b_ref[span, :],
-            (((1,), (1,)), ((), ())),
-            preferred_element_type=F32,
-        )
-        x_ref[span, 0:STEP] = jnp.where(row_i >= col_i, scores, 0.0).astype(BF16)
-        x_ref[span, STEP:] = c_ref[span, :]
+
+    def prepare_outputs():
+        g_copy.wait()
+        c_copy.wait()
+        gain_copy.wait()
+        offset = jnp.zeros((heads, 1), F32)
+        for c in range(steps):
+            span = slice(c * STEP, (c + 1) * STEP)
+            run = run_of(c)
+            put_weight(1, span, g_ref[0, :, span] * jnp.exp(run - 0.5 * last_columns[c]))
+            cum_exp = jnp.exp(run + offset)
+            for bit in range(bits):
+                put_weight(2 + bit, span, g_ref[bit + 1, :, span] * cum_exp)
+            offset = offset + last_columns[c]
+            scores = lax.dot_general(
+                c_ref[span, :],
+                b_ref[span, :],
+                (((1,), (1,)), ((), ())),
+                preferred_element_type=F32,
+            )
+            x_ref[span, 0:STEP] = jnp.where(row_i >= col_i, scores, 0.0).astype(BF16)
+            x_ref[span, STEP:] = c_ref[span, :]
+
     step_logs = jnp.concatenate(
         [jnp.broadcast_to(last, (heads, STEP)) for last in last_columns], axis=0
     )
@@ -328,7 +364,12 @@
                 combined * lax.rsqrt(mean_square + 1e-05) * gain
             ).astype(BF16)
 
+    def out_copy(q):
+        span = pl.ds(q * LANES, LANES)
+        return pltpu.make_async_copy(o_ref.at[:, span], o_hbm.at[:, span], out_sem.at[q])
+
     for q in range(chunks):
+        v_copies[q].wait()
         near(q)
         if q == 0:
             below = (outer + n_outer - 1) // n_outer
@@ -337,6 +378,7 @@
         start_first(q, 0)
     for q in range(chunks):
         start_first(q, 1)
+    prepare_outputs()
     events = []
     for level in range(bits):
         for late in range(2):
@@ -352,10 +394,19 @@
             pl.when(needs(level))(lambda: far(level, q))
             if level == bits - 1:
                 finish(q)
+                out_copy(q).start()
     for level in range(bits):
         for late in range(2):
             for q in range(chunks):
                 wait_sent(level, q, late)
+    for q in range(chunks):
+        out_copy(q).wait()
+
+
+def hand_over(source, target, sem):
+    copy = pltpu.make_async_copy(source, target, sem)
+    copy.start()
+    copy.wait()
 
 
 def per_device(n_outer, n_inner, values, input_state, output_state, decay, gates, gain):
@@ -365,13 +416,21 @@
     steps, chunks = tokens // STEP, width // LANES
     units = width // UNIT
     flight = (bits, units, N + 8, UNIT)
-    in_vmem = pl.BlockSpec(memory_space=pltpu.VMEM)
-    return pl.pallas_call(
+    in_hbm = pl.BlockSpec(memory_space=pltpu.HBM)
+    anywhere = pl.BlockSpec(memory_space=pl.ANY)
+    mixed = pl.pallas_call(
         functools.partial(kernel, n_outer, n_inner),
         out_shape=jax.ShapeDtypeStruct((tokens, width), BF16),
-        in_specs=[in_vmem] * 6,
-        out_specs=in_vmem,
+        in_specs=[in_hbm] * 6,
+        out_specs=anywhere,
         scratch_shapes=[
+            pltpu.VMEM((tokens, width), BF16),
+            pltpu.VMEM(input_state.shape, BF16),
+            pltpu.VMEM(decay.shape, F32),
+            pltpu.VMEM((1, width), F32),
+            pltpu.VMEM(output_state.shape, BF16),
+            pltpu.VMEM(gates.shape, F32),
+            pltpu.VMEM((tokens, width), BF16),
             pltpu.VMEM((2 + bits, tokens, 2 * heads), BF16),
             pltpu.VMEM((2 * heads, width), BF16),
             pltpu.VMEM((steps, N, STEP), BF16),
@@ -385,11 +444,21 @@
             pltpu.SemaphoreType.DMA((bits, units)),
             pltpu.SemaphoreType.DMA((bits, units)),
             pltpu.SemaphoreType.DMA((bits, units)),
+            pltpu.SemaphoreType.DMA((chunks + 5,)),
+            pltpu.SemaphoreType.DMA((chunks,)),
         ],
         compiler_params=pltpu.CompilerParams(
             collective_id=0, has_side_effects=True, vmem_limit_bytes=56 * 1024 * 1024
         ),
     )(values, input_state, output_state, decay, gates, gain.reshape(1, width))
+    return pl.pallas_call(
+        hand_over,
+        out_shape=jax.ShapeDtypeStruct((tokens, width), BF16),
+        in_specs=[anywhere],
+        out_specs=anywhere,
+        scratch_shapes=[pltpu.SemaphoreType.DMA],
+        compiler_params=pltpu.CompilerParams(vmem_limit_bytes=1024 * 1024),
+    )(mixed)
 
 
 def solution(mesh):

time: 34.6 us -> 33.2 us (0.960)
  local copies, waits for them, and re-layouts: 3.08 us -> 1.58 us
    unnamed x1 -> x2, local copies, waits for them, and re-layouts: 3.08 us -> 1.58 us
    pallas_call x0 -> x1, Pallas kernels: none -> 1.33 us  [per_device(): pl.pallas_call(hand_over, out_shape=jax.ShapeDtypeStruct((tokens, width),...]
    pallas_call x1, Pallas kernels: 31.3 us -> 30.1 us  [per_device(): pl.pallas_call(functools.partial(kernel, n_outer, n_inner), out_shape=jax...]
where the time goes in v3:
time: 33.2 us; the launch traced here: 33.1 us
  Pallas kernels  31.5 us (95%)
  local copies, waits for them, and re-layouts  1.58 us (5%)
    pallas_call x1, Pallas kernels, per_device(): pl.pallas_call(functools.partial(kernel, n_outer, n_inner), out_shape=jax...  30.1 us
    unnamed x2, local copies, waits for them, and re-layouts  1.58 us
    pallas_call x1, Pallas kernels, per_device(): pl.pallas_call(hand_over, out_shape=jax.ShapeDtypeStruct((tokens, width),...  1.33 us

profile of v3, /device:TPU:26, one launch (start us, length us, event | category | flops | bytes accessed | tf_op | source)
XLA Modules:
  0.0 33.1 jit_solution(14666478154200516734)
XLA Ops:
  0.0 30.1 %shard_map.64.source = bf16[1024,1024]{1,0:T(8,128)(2,1)} custom-call(bf16[1024,1024]{1,0:T(8,128)(2,1)} %v_hbm.1, bf16[1024,128]{1,0:T(8,128)(2,1)} %b_hbm.1, bf16[1024,128]{1,0:T(8,128)(2,1)} %c_hbm.1, f32[16,1024]{1,0:T(8,128)} %d_hbm.1, f32[4,16,1024]{2,1,0:T(8,128)} %g_hbm.1, f32[1,1024]{1,0:T(1,128)} %bitcast.1), custom_call_target="tpu_custom_call" | custom-call | tf_op jit(solution)/shard_map/pallas_call | solution.py:421
  30.1 0.0 copy-start
  30.2 1.6 %copy-done = bf16[1024,1024]{1,0:T(8,128)(2,1)S(1)} copy-done((bf16[1024,1024]{1,0:T(8,128)(2,1)S(1)}, bf16[1024,1024]{1,0:T(8,128)(2,1)}, u32[]{:S(2)}) %copy-start) | copy-done | bytes 2097176
  31.7 1.3 %shard_map.65 = bf16[1024,1024]{1,0:T(8,128)(2,1)} custom-call(bf16[1024,1024]{1,0:T(8,128)(2,1)S(1)} %copy-done), custom_call_target="tpu_custom_call" | custom-call | tf_op jit(solution)/shard_map/pallas_call | solution.py:454
Async XLA Ops:
  30.1 1.6 %copy-start = (bf16[1024,1024]{1,0:T(8,128)(2,1)S(1)}, bf16[1024,1024]{1,0:T(8,128)(2,1)}, u32[]{:S(2)}) copy-start(bf16[1024,1024]{1,0:T(8,128)(2,1)} %shard_map.64.source) | copy-start | bytes 6291460
